TPU v7x, 32 devices: a whole 2x2x4 slice. The times are simulated.
32 devices in a mesh: row: 4 (over y, x), col: 8 (over z, core).
Axes of the slice: x: 2, y: 2, z: 4, core: 2. Of those that a mesh axis runs over, the one named last changes fastest.
Arguments:
- points: bfloat16 [8192, 256], P(('row', 'col')), may hold values from -0.4 to 0.4, as said below
- spread: float32 [8192], P(('row', 'col')), may hold values from 1 to 12
- vectors: bfloat16 [8192, 64], P(('row', 'col')), may hold values from -6 to 6
Outputs:
- product: float32 [8192, 64], P(('row', 'col'))
Inputs may be any that keep to these rules, and one draw needn't show every extreme that they name: `points`: embedding entries are real values of order 0.1.
All inputs are finite; a program needn't handle non-finite values.
Results may differ from a plain program's by a relative error of at most 0.0085.
Values may be sent and summed in bfloat16 or wider, within the bound.
A program may use at most 128 MiB of HBM per device.

v0:
```python
import jax
import jax.numpy as jnp
from jax import lax
from jax.sharding import PartitionSpec as P


def distances(left_pts, right_pts):
    left_f = left_pts.astype(jnp.float32)
    right_f = right_pts.astype(jnp.float32)
    left_sq = jnp.sum(left_f * left_f, axis=1)
    right_sq = jnp.sum(right_f * right_f, axis=1)
    cross = lax.dot_general(
        left_pts, right_pts, (((1,), (1,)), ((), ())), preferred_element_type=jnp.float32
    )
    return left_sq[:, None] + right_sq[None, :] - 2.0 * cross


def local(points, spread, vectors):
    share_rows = points.shape[0]
    n_rows = lax.axis_size("row")
    n_cols = lax.axis_size("col")
    row_pos = lax.axis_index("row")
    col_pos = lax.axis_index("col")
    blk_pts, blk_bw, blk_vec = (
        lax.all_gather(points, "col", axis=0, tiled=True),
        lax.all_gather(spread.astype(jnp.bfloat16), "col", axis=0, tiled=True).astype(spread.dtype),
        lax.all_gather(vectors, "col", axis=0, tiled=True),
    )
    crs_pts, crs_bw, crs_vec = (
        lax.all_gather(points, "row", axis=0, tiled=True),
        lax.all_gather(spread.astype(jnp.bfloat16), "row", axis=0, tiled=True).astype(spread.dtype),
        lax.all_gather(vectors, "row", axis=0, tiled=True),
    )
    blk_local = jnp.arange(share_rows * n_cols, dtype=jnp.int32)
    blk_ids = row_pos * (n_cols * share_rows) + blk_local
    crs_local = jnp.arange(share_rows * n_rows, dtype=jnp.int32)
    crs_ids = (
        crs_local // share_rows * (n_cols * share_rows)
        + col_pos * share_rows
        + crs_local % share_rows
    )
    same = blk_ids[:, None] == crs_ids[None, :]
    dist = distances(blk_pts, crs_pts)
    kernel = jnp.where(same, jnp.float32(0.0), jnp.exp(-blk_bw[:, None] * dist))
    totals = lax.psum(jnp.sum(kernel, axis=1), "col")
    norm = (kernel / totals[:, None]).astype(jnp.bfloat16)
    to_cross = lax.dot_general(
        norm, blk_vec, (((0,), (0,)), ((), ())), preferred_element_type=jnp.float32
    )
    mirror = jnp.where(same, jnp.float32(0.0), jnp.exp(-crs_bw[None, :] * dist))
    mirror_tot = lax.psum(jnp.sum(mirror, axis=0), "row")
    mirror_norm = (mirror / mirror_tot[None, :]).astype(jnp.bfloat16)
    to_cross = to_cross + lax.dot_general(
        mirror_norm, blk_vec, (((0,), (0,)), ((), ())), preferred_element_type=jnp.float32
    )
    summed = lax.psum_scatter(to_cross, "row", scatter_dimension=0, tiled=True)
    return 0.5 * summed


def solution(mesh):
    placed = (P(("row", "col"), None), P(("row", "col")), P(("row", "col"), None))
    return jax.shard_map(
        local, mesh=mesh, in_specs=placed, out_specs=P(("row", "col"), None), check_vma=False
    )
```

profile of v0, /device:TPU:0, one launch (start us, length us, event | category | flops | bytes accessed | tf_op | source)
XLA Modules:
  0.0 126.9 jit_solution(6512187139585747209)
XLA Ops:
  6.5 0.0 all-gather.4.cloned.1.call-start
  6.5 0.7 all-gather.4.cloned.1.call-update
  7.3 0.0 reduce-scatter.2.cloned.1.call-start
  7.3 0.7 convert_element_type.22
  8.0 9.5 %all-gather.1 = bf16[4,1,256]{2,1,0:T(2,128)(2,1)S(1)} all-gather(bf16[1,1,256]{2,1,0:T(2,128)(2,1)S(1)} %reshape.35), channel_id=1, replica_groups=mesh['row'=4,'col'=8] {'row'}, dimensions={0}, use_global_device_ids=true | all-gather | bytes 2560 | tf_op jit(solution)/shard_map/all_gather | solution.py:31
  17.5 12.0 %all-gather = bf16[8,1,256]{2,1,0:T(2,128)(2,1)S(1)} all-gather(bf16[1,1,256]{2,1,0:T(2,128)(2,1)S(1)} %reshape.35), channel_id=1, replica_groups=mesh['row'=4,'col'=8] {'col'}, dimensions={0}, use_global_device_ids=true | all-gather | bytes 4608 | tf_op jit(solution)/shard_map/all_gather | solution.py:26
  29.5 10.3 %all_gather.17 = bf16[1024,256]{1,0:T(8,128)(2,1)S(1)} all-gather(bf16[256,256]{1,0:T(8,128)(2,1)} %param.3), channel_id=1, replica_groups=mesh['row'=4,'col'=8] {'row'}, dimensions={0}, use_global_device_ids=true | all-gather | bytes 655360 | tf_op jit(solution)/shard_map/all_gather | solution.py:30
  39.8 14.4 %all_gather.18 = bf16[2048,64]{0,1:T(8,128)(2,1)S(1)} all-gather(bf16[256,64]{0,1:T(8,128)(2,1)} %param.5), channel_id=1, replica_groups=mesh['row'=4,'col'=8] {'col'}, dimensions={0}, use_global_device_ids=true | all-gather | bytes 294912 | tf_op jit(solution)/shard_map/all_gather | solution.py:27
  54.2 0.2 multiply_reduce_fusion.1
  54.5 0.0 all-gather.4.cloned.1.call-done
  54.5 1.6 %multiply_reduce_fusion = f32[2048]{0:T(1024)S(1)} fusion(bf16[2048,256]{1,0:T(8,128)(2,1)} %all-gather.4.cloned.1.call-done), kind=kLoop, calls=%fused_computation.9 | loop fusion | flops 1570816 | bytes 1056768 | tf_op jit(solution)/shard_map/reduce_sum | solution.py:10
  56.1 7.5 %fusion = (f32[2048]{0:T(1024)S(1)}, f32[1024]{0:T(1024)S(1)}, f32[2048,1024]{1,0:T(8,128)}) fusion(f32[1024]{0:T(1024)S(1)} %multiply_reduce_fusion.1, f32[2048]{0:T(1024)S(1)} %multiply_reduce_fusion, f32[2048]{0:T(1024)S(1)} %bitcast.6, s32[1024]{0:T(1024)S(1)} %fusion.13, s32[2048]{0:T(1024)S(1)} %iota_add_fusion, f32[1024]{0:T(1024)S(1)} %bitcast.8, ...), kind=kOutput, calls=%fused_computation.5 | convolution fusion | flops 1094710272 | bytes 10010624 | tf_op jit(solution)/shard_map/dot_general | solution.py:12
  63.6 8.9 %psum.15 = f32[1024]{0:T(1024)S(1)} all-reduce(f32[1024]{0:T(1024)S(1)} %get-tuple-element.6), channel_id=1, replica_groups=mesh['row'=4,'col'=8] {'row'}, use_global_device_ids=true, to_apply=%region_5.6 | all-reduce | flops 1024 | bytes 8192 | tf_op jit(solution)/shard_map/psum | solution.py:51
  72.5 13.9 %psum.14 = f32[2048]{0:T(1024)S(1)} all-reduce(f32[2048]{0:T(1024)S(1)} %get-tuple-element.5), channel_id=1, replica_groups=mesh['row'=4,'col'=8] {'col'}, use_global_device_ids=true, to_apply=%region_3.4 | all-reduce | flops 2048 | bytes 16384 | tf_op jit(solution)/shard_map/psum | solution.py:45
  86.4 0.0 copy-start
  86.4 6.9 %fusion.2 = f32[1024,64]{0,1:T(8,128)S(1)} fusion(bf16[2048,64]{0,1:T(8,128)(2,1)S(1)} %all_gather.18, f32[2048,1024]{1,0:T(8,128)} %get-tuple-element.7, f32[1024]{0:T(1024)S(1)} %psum.15, f32[1024]{0:T(1024)S(1)} %bitcast.9, f32[1024]{0:T(1024)S(1)} %multiply_reduce_fusion.1, f32[2048]{0:T(1024)S(1)} %multiply_reduce_fusion, s32[1024]{0:T(1024)S(1)} %fusion.13, ...), kind=kOutput, calls=%fused_computation.7 | convolution fusion | flops 285212672 | bytes 8945664 | tf_op jit(solution)/shard_map/dot_general | solution.py:53
  93.3 0.0 copy-done
  93.3 3.8 %fusion.4 = f32[1024,64]{0,1:T(8,128)} fusion(f32[1024,64]{0,1:T(8,128)S(1)} %fusion.2, bf16[2048,64]{0,1:T(8,128)(2,1)S(1)} %all_gather.18, f32[2048,1024]{1,0:T(8,128)S(1)} %copy-done, f32[2048]{0:T(1024)S(1)} %psum.14, f32[1024]{0:T(1024)S(1)} %multiply_reduce_fusion.1, f32[2048]{0:T(1024)S(1)} %multiply_reduce_fusion, f32[2048]{0:T(1024)S(1)} %bitcast.7, ...), kind=kOutput, calls=%fused_computation.10 | convolution fusion | flops 285278208 | bytes 9216000 | tf_op jit(solution)/shard_map/dot_general | solution.py:47
  97.1 0.0 reduce-scatter.2.cloned.1.call-update
  97.2 21.5 %reduce-scatter.2.cloned.1.call-done = f32[256,64]{0,1:T(8,128)} async-done(((f32[1024,64]{0,1:T(8,128)}), f32[256,64]{0,1:T(8,128)}) %reduce-scatter.2.cloned.1.call-update) | async-done | bytes 65552 | tf_op jit(solution)/shard_map/reduce_scatter | solution.py:56
  118.6 1.5 %broadcast_multiply_fusion = f32[256,64]{0,1:T(8,128)} fusion(f32[256,64]{0,1:T(8,128)} %reduce-scatter.2.cloned.1.call-done), kind=kLoop, calls=%fused_computation.12 | loop fusion | flops 16384 | bytes 131072 | tf_op jit(solution)/shard_map/mul | solution.py:57
  (5 shorter events, 0.0 us)
Async XLA Ops:
  6.5 47.9 %all-gather.4.cloned.1.call-start = ((), (), s32[]{:S(2)}) async-start(), calls=%async_computation.1 | async-start | bytes 1179648 | tf_op jit(solution)/shard_map/all_gather | solution.py:25
  7.3 111.4 %reduce-scatter.2.cloned.1.call-start = ((), (), s32[]{:S(2)}) async-start(), calls=%async_computation.2 | async-start | bytes 327680 | tf_op jit(solution)/shard_map/reduce_scatter | solution.py:56
  86.4 6.9 %copy-start = (f32[2048,1024]{1,0:T(8,128)S(1)}, f32[2048,1024]{1,0:T(8,128)}, u32[]{:S(2)}) copy-start(f32[2048,1024]{1,0:T(8,128)} %get-tuple-element.7) | copy-start | bytes 25165828
Sparse Core Ops, SparseCore 0:
  9.0 24.7 all-gather.3
  97.3 21.3 reduce-scatter.1
where the time goes:
time: 127 us
  blocking collectives  69 us (54%)
  waiting for transfers between devices  22.2 us (17%)
  matrix products  18.2 us (14%)
  between operations  13.5 us (11%)
  other arithmetic  3.97 us (3%)
    reduce_scatter x1, waiting for transfers between devices, local(): summed = lax.psum_scatter(to_cross, 'row', scatter_dimension=0, tiled=True)  21.5 us
    all_gather x1, blocking collectives, local(): lax.all_gather(vectors, 'col', axis=0, tiled=True)  14.4 us
    psum x1, blocking collectives, local(): totals = lax.psum(jnp.sum(kernel, axis=1), 'col')  13.9 us
    all_gather x1, blocking collectives, local(): lax.all_gather(spread.astype(jnp.bfloat16), 'col', axis=0, tiled=True)  12 us
    all_gather x1, blocking collectives, local(): lax.all_gather(points, 'row', axis=0, tiled=True)  10.3 us
    all_gather x1, blocking collectives, local(): lax.all_gather(spread.astype(jnp.bfloat16), 'row', axis=0, tiled=True)  9.5 us
    psum x1, blocking collectives, local(): mirror_tot = lax.psum(jnp.sum(mirror, axis=0), 'row')  8.9 us
    dot_general x1, matrix products, distances(): lax.dot_general(left_pts, right_pts, (((1,), (1,)), ((), ())), preferred_...  7.5 us
  transfers between devices with their start and end apart: 2, of which 1 were waited for; matrix products, arithmetic and copies ran while one was open for 1% of the time, Pallas kernels for 0%

commit v1 on v0

--- a/solution.py
+++ b/solution.py
@@ -2,6 +2,22 @@
 import jax.numpy as jnp
 from jax import lax
 from jax.sharding import PartitionSpec as P
+
+
+def gather_around(x, axis, dim):
+    ways, here, lap = (lax.axis_size(axis), lax.axis_index(axis), x.shape[dim])
+    shape = [n * ways if d == dim else n for d, n in enumerate(x.shape)]
+    full = lax.dynamic_update_slice_in_dim(jnp.zeros(shape, x.dtype), x, here * lap, axis=dim)
+    going_up = going_down = x
+    for far in range(1, ways // 2 + 1):
+        going_up = lax.ppermute(going_up, axis, [(d, (d + 1) % ways) for d in range(ways)])
+        full = lax.dynamic_update_slice_in_dim(full, going_up, (here - far) % ways * lap, axis=dim)
+        if 2 * far < ways:
+            going_down = lax.ppermute(going_down, axis, [(d, (d - 1) % ways) for d in range(ways)])
+            full = lax.dynamic_update_slice_in_dim(
+                full, going_down, (here + far) % ways * lap, axis=dim
+            )
+    return full
 
 
 def distances(left_pts, right_pts):
@@ -23,7 +39,7 @@
     col_pos = lax.axis_index("col")
     blk_pts, blk_bw, blk_vec = (
         lax.all_gather(points, "col", axis=0, tiled=True),
-        lax.all_gather(spread.astype(jnp.bfloat16), "col", axis=0, tiled=True).astype(spread.dtype),
+        gather_around(spread.astype(jnp.bfloat16), "col", 0).astype(spread.dtype),
         lax.all_gather(vectors, "col", axis=0, tiled=True),
     )
     crs_pts, crs_bw, crs_vec = (

time: 127 us -> 132 us (1.039)
  blocking collectives: 69 us -> 55.8 us
  starting transfers between devices: 0.04 us -> 11.7 us
  waiting for transfers between devices: 22.2 us -> 27.4 us
  local copies, waits for them, and re-layouts: 0.01 us -> 1.61 us
    all_gather x1 -> x0, blocking collectives: 12 us -> none  [local(): lax.all_gather(spread.astype(jnp.bfloat16), 'col', axis=0, tiled=True)]
    ppermute x0 -> x7, starting transfers between devices: none -> 11.6 us  [the longest x3 10.8 us: gather_around(): lax.ppermute(going_down, axis, [(d, (d - 1) % ways) for d in range(ways)])]
    ppermute x0 -> x7, waiting for transfers between devices: none -> 5.78 us  [the longest x4 5.77 us: gather_around(): lax.ppermute(going_up, axis, [(d, (d + 1) % ways) for d in range(ways)])]
    dynamic_update_slice x0 -> x8, local copies, waits for them, and re-layouts: none -> 1.6 us  [the longest x4 0.75 us: gather_around(): lax.dynamic_update_slice_in_dim(full, going_up, (here - far) % ways * lap...]
  transfers between devices with their start and end apart: 2 -> 9, of which waited for: 1 -> 4; matrix products, arithmetic and copies ran while one was open for 1% -> 2% of each run, Pallas kernels for 0% -> 0%
where the time goes in v1:
time: 132 us
  blocking collectives  55.8 us (42%)
  waiting for transfers between devices  27.4 us (21%)
  matrix products  18.1 us (14%)
  between operations  13.5 us (10%)
  starting transfers between devices  11.7 us (9%)
  other arithmetic  3.96 us (3%)
  local copies, waits for them, and re-layouts  1.61 us (1%)
    reduce_scatter x1, waiting for transfers between devices, local(): summed = lax.psum_scatter(to_cross, 'row', scatter_dimension=0, tiled=True)  20.9 us
    all_gather x1, blocking collectives, local(): lax.all_gather(vectors, 'col', axis=0, tiled=True)  14.4 us
    psum x1, blocking collectives, local(): totals = lax.psum(jnp.sum(kernel, axis=1), 'col')  13.9 us
    ppermute x3, starting transfers between devices, gather_around(): lax.ppermute(going_down, axis, [(d, (d - 1) % ways) for d in range(ways)])  10.8 us
    all_gather x1, blocking collectives, local(): lax.all_gather(points, 'row', axis=0, tiled=True)  10 us
    psum x1, blocking collectives, local(): mirror_tot = lax.psum(jnp.sum(mirror, axis=0), 'row')  8.89 us
    all_gather x1, blocking collectives, local(): lax.all_gather(spread.astype(jnp.bfloat16), 'row', axis=0, tiled=True)  8.56 us
    dot_general x1, matrix products, distances(): lax.dot_general(left_pts, right_pts, (((1,), (1,)), ((), ())), preferred_...  7.48 us
  transfers between devices with their start and end apart: 9, of which 4 were waited for; matrix products, arithmetic and copies ran while one was open for 2% of the time, Pallas kernels for 0%

profile of v1, /device:TPU:0, one launch (start us, length us, event | category | flops | bytes accessed | tf_op | source)
XLA Modules:
  0.0 132.0 jit_solution(7380711199094519799)
XLA Ops:
  6.5 0.0 all-gather.3.cloned.1.call-start
  6.5 0.7 all-gather.3.cloned.1.call-update
  7.3 0.0 reduce-scatter.2.cloned.1.call-start
  7.3 0.7 convert_element_type.22
  8.0 0.5 collective-permute-start
  8.4 4.0 %collective-permute-start.1 = (bf16[256]{0:T(256)(128)(2,1)S(1)}, bf16[256]{0:T(256)(128)(2,1)S(1)}, u32[]{:S(2)}, u32[]{:S(2)}) collective-permute-start(bf16[256]{0:T(256)(128)(2,1)S(1)} %convert_element_type.22), channel_id=1, source_target_pairs={{0,7},{1,0},{2,1},{3,2},{4,3},{5,4},{6,5},{7,6},{8,15},{9,8},{10,9... | collective-permute-start | bytes 1544 | tf_op jit(solution)/shard_map/ppermute | solution.py:16
  12.5 8.6 %all-gather = bf16[4,1,256]{2,1,0:T(2,128)(2,1)S(1)} all-gather(bf16[1,1,256]{2,1,0:T(2,128)(2,1)S(1)} %reshape.35), channel_id=1, replica_groups=mesh['row'=4,'col'=8] {'row'}, dimensions={0}, use_global_device_ids=true | all-gather | bytes 2560 | tf_op jit(solution)/shard_map/all_gather | solution.py:47
  21.0 10.0 %all_gather.13 = bf16[1024,256]{1,0:T(8,128)(2,1)S(1)} all-gather(bf16[256,256]{1,0:T(8,128)(2,1)} %param.3), channel_id=1, replica_groups=mesh['row'=4,'col'=8] {'row'}, dimensions={0}, use_global_device_ids=true | all-gather | bytes 655360 | tf_op jit(solution)/shard_map/all_gather | solution.py:46
  31.1 14.4 %all_gather.14 = bf16[2048,64]{0,1:T(8,128)(2,1)S(1)} all-gather(bf16[256,64]{0,1:T(8,128)(2,1)} %param.5), channel_id=1, replica_groups=mesh['row'=4,'col'=8] {'col'}, dimensions={0}, use_global_device_ids=true | all-gather | bytes 294912 | tf_op jit(solution)/shard_map/all_gather | solution.py:43
  45.5 0.2 multiply_reduce_fusion.1
  45.7 0.0 collective-permute-done
  45.7 0.4 collective-permute-start.2
  46.1 0.0 collective-permute-done.1
  46.1 3.2 %collective-permute-start.3 = (bf16[256]{0:T(256)(128)(2,1)S(1)}, bf16[256]{0:T(256)(128)(2,1)S(1)}, u32[]{:S(2)}, u32[]{:S(2)}) collective-permute-start(bf16[256]{0:T(256)(128)(2,1)S(1)} %collective-permute-done.1), channel_id=1, source_target_pairs={{0,7},{1,0},{2,1},{3,2},{4,3},{5,4},{6,5},{7,6},{8,15},{9,8},{10,9... | collective-permute-start | bytes 1544 | tf_op jit(solution)/shard_map/ppermute | solution.py:16
  49.3 1.2 collective-permute-done.2
  50.5 0.0 collective-permute-start.4
  50.6 0.2 dynamic_update_slice.24
  50.8 0.0 collective-permute-done.3
  50.8 3.5 %collective-permute-start.5 = (bf16[256]{0:T(256)(128)(2,1)S(1)}, bf16[256]{0:T(256)(128)(2,1)S(1)}, u32[]{:S(2)}, u32[]{:S(2)}) collective-permute-start(bf16[256]{0:T(256)(128)(2,1)S(1)} %collective-permute-done.3), channel_id=1, source_target_pairs={{0,7},{1,0},{2,1},{3,2},{4,3},{5,4},{6,5},{7,6},{8,15},{9,8},{10,9... | collective-permute-start | bytes 1544 | tf_op jit(solution)/shard_map/ppermute | solution.py:16
  54.3 1.0 collective-permute-done.4
  55.3 0.0 collective-permute-start.6
  55.3 0.2 dynamic_update_slice.25
  55.5 0.2 dynamic_update_slice.26
  55.7 0.2 dynamic_update_slice.27
  55.9 0.2 dynamic_update_slice.28
  56.1 0.2 dynamic_update_slice.29
  56.3 0.0 collective-permute-done.5
  56.3 0.2 dynamic_update_slice.30
  56.5 3.6 %collective-permute-done.6 = bf16[256]{0:T(256)(128)(2,1)S(1)} collective-permute-done((bf16[256]{0:T(256)(128)(2,1)S(1)}, bf16[256]{0:T(256)(128)(2,1)S(1)}, u32[]{:S(2)}, u32[]{:S(2)}) %collective-permute-start.6) | collective-permute-done | bytes 544 | tf_op jit(solution)/shard_map/ppermute | solution.py:13
  60.1 0.2 dynamic_update_slice.31
  60.3 0.0 all-gather.3.cloned.1.call-done
  60.3 1.6 %multiply_reduce_fusion = f32[2048]{0:T(1024)S(1)} fusion(bf16[2048,256]{1,0:T(8,128)(2,1)} %all-gather.3.cloned.1.call-done), kind=kLoop, calls=%fused_computation.9 | loop fusion | flops 1570816 | bytes 1056768 | tf_op jit(solution)/shard_map/reduce_sum | solution.py:26
  61.8 7.5 %fusion = (f32[2048]{0:T(1024)S(1)}, f32[1024]{0:T(1024)S(1)}, f32[2048,1024]{1,0:T(8,128)}) fusion(f32[1024]{0:T(1024)S(1)} %multiply_reduce_fusion.1, f32[2048]{0:T(1024)S(1)} %multiply_reduce_fusion, f32[2048]{0:T(1024)S(1)} %convert_negate_fusion, s32[1024]{0:T(1024)S(1)} %fusion.13, s32[2048]{0:T(1024)S(1)} %iota_add_fusion, f32[1024]{0:T(1024)S(1)} %bitcast.5, ...), kind=kOutput, calls=%fused_computation.5 | convolution fusion | flops 1094710272 | bytes 10010624 | tf_op jit(solution)/shard_map/dot_general | solution.py:28
  69.3 8.9 %psum.15 = f32[1024]{0:T(1024)S(1)} all-reduce(f32[1024]{0:T(1024)S(1)} %get-tuple-element.6), channel_id=1, replica_groups=mesh['row'=4,'col'=8] {'row'}, use_global_device_ids=true, to_apply=%region_5.6 | all-reduce | flops 1024 | bytes 8192 | tf_op jit(solution)/shard_map/psum | solution.py:67
  78.2 13.9 %psum.14 = f32[2048]{0:T(1024)S(1)} all-reduce(f32[2048]{0:T(1024)S(1)} %get-tuple-element.5), channel_id=1, replica_groups=mesh['row'=4,'col'=8] {'col'}, use_global_device_ids=true, to_apply=%region_3.4 | all-reduce | flops 2048 | bytes 16384 | tf_op jit(solution)/shard_map/psum | solution.py:61
  92.1 0.0 copy-start
  92.1 6.9 %fusion.2 = f32[1024,64]{0,1:T(8,128)S(1)} fusion(bf16[2048,64]{0,1:T(8,128)(2,1)S(1)} %all_gather.14, f32[2048,1024]{1,0:T(8,128)} %get-tuple-element.7, f32[1024]{0:T(1024)S(1)} %psum.15, f32[1024]{0:T(1024)S(1)} %bitcast.6, f32[1024]{0:T(1024)S(1)} %multiply_reduce_fusion.1, f32[2048]{0:T(1024)S(1)} %multiply_reduce_fusion, s32[1024]{0:T(1024)S(1)} %fusion.13, ...), kind=kOutput, calls=%fused_computation.7 | convolution fusion | flops 285212672 | bytes 8945664 | tf_op jit(solution)/shard_map/dot_general | solution.py:69
  99.1 0.0 copy-done
  99.1 3.7 %fusion.4 = f32[1024,64]{0,1:T(8,128)} fusion(f32[1024,64]{0,1:T(8,128)S(1)} %fusion.2, bf16[2048,64]{0,1:T(8,128)(2,1)S(1)} %all_gather.14, f32[2048,1024]{1,0:T(8,128)S(1)} %copy-done, f32[2048]{0:T(1024)S(1)} %psum.14, f32[1024]{0:T(1024)S(1)} %multiply_reduce_fusion.1, f32[2048]{0:T(1024)S(1)} %multiply_reduce_fusion, f32[2048]{0:T(1024)S(1)} %convert_negate_fusion, ...), kind=kOutput, calls=%fused_computation.10 | convolution fusion | flops 285278208 | bytes 9216000 | tf_op jit(solution)/shard_map/dot_general | solution.py:63
  102.8 0.0 reduce-scatter.2.cloned.1.call-update
  102.8 20.9 %reduce-scatter.2.cloned.1.call-done = f32[256,64]{0,1:T(8,128)} async-done(((f32[1024,64]{0,1:T(8,128)}), f32[256,64]{0,1:T(8,128)}) %reduce-scatter.2.cloned.1.call-update) | async-done | bytes 65552 | tf_op jit(solution)/shard_map/reduce_scatter | solution.py:72
  123.7 1.5 %broadcast_multiply_fusion = f32[256,64]{0,1:T(8,128)} fusion(f32[256,64]{0,1:T(8,128)} %reduce-scatter.2.cloned.1.call-done), kind=kLoop, calls=%fused_computation.12 | loop fusion | flops 16384 | bytes 131072 | tf_op jit(solution)/shard_map/mul | solution.py:73
  (6 shorter events, 0.0 us)
Async XLA Ops:
  6.5 53.7 %all-gather.3.cloned.1.call-start = ((), (), s32[]{:S(2)}) async-start(), calls=%async_computation.1 | async-start | bytes 1179648 | tf_op jit(solution)/shard_map/all_gather | solution.py:41
  7.3 116.5 %reduce-scatter.2.cloned.1.call-start = ((), (), s32[]{:S(2)}) async-start(), calls=%async_computation.2 | async-start | bytes 327680 | tf_op jit(solution)/shard_map/reduce_scatter | solution.py:72
  8.0 37.7 %collective-permute-start = (bf16[256]{0:T(256)(128)(2,1)S(1)}, bf16[256]{0:T(256)(128)(2,1)S(1)}, u32[]{:S(2)}, u32[]{:S(2)}) collective-permute-start(bf16[256]{0:T(256)(128)(2,1)S(1)} %convert_element_type.22), channel_id=1, source_target_pairs={{0,1},{1,2},{2,3},{3,4},{4,5},{5,6},{6,7},{7,0},{8,9},{9,10},{10,1... | collective-permute-start | bytes 1544 | tf_op jit(solution)/shard_map/ppermute | solution.py:13
  8.4 37.7 %collective-permute-start.1 = (bf16[256]{0:T(256)(128)(2,1)S(1)}, bf16[256]{0:T(256)(128)(2,1)S(1)}, u32[]{:S(2)}, u32[]{:S(2)}) collective-permute-start(bf16[256]{0:T(256)(128)(2,1)S(1)} %convert_element_type.22), channel_id=1, source_target_pairs={{0,7},{1,0},{2,1},{3,2},{4,3},{5,4},{6,5},{7,6},{8,15},{9,8},{10,9... | collective-permute-start | bytes 1544 | tf_op jit(solution)/shard_map/ppermute | solution.py:16
  45.7 4.8 %collective-permute-start.2 = (bf16[256]{0:T(256)(128)(2,1)S(1)}, bf16[256]{0:T(256)(128)(2,1)S(1)}, u32[]{:S(2)}, u32[]{:S(2)}) collective-permute-start(bf16[256]{0:T(256)(128)(2,1)S(1)} %collective-permute-done), channel_id=1, source_target_pairs={{0,1},{1,2},{2,3},{3,4},{4,5},{5,6},{6,7},{7,0},{8,9},{9,10},{10,1... | collective-permute-start | bytes 1544 | tf_op jit(solution)/shard_map/ppermute | solution.py:13
  46.1 4.7 %collective-permute-start.3 = (bf16[256]{0:T(256)(128)(2,1)S(1)}, bf16[256]{0:T(256)(128)(2,1)S(1)}, u32[]{:S(2)}, u32[]{:S(2)}) collective-permute-start(bf16[256]{0:T(256)(128)(2,1)S(1)} %collective-permute-done.1), channel_id=1, source_target_pairs={{0,7},{1,0},{2,1},{3,2},{4,3},{5,4},{6,5},{7,6},{8,15},{9,8},{10,9... | collective-permute-start | bytes 1544 | tf_op jit(solution)/shard_map/ppermute | solution.py:16
  50.5 4.8 %collective-permute-start.4 = (bf16[256]{0:T(256)(128)(2,1)S(1)}, bf16[256]{0:T(256)(128)(2,1)S(1)}, u32[]{:S(2)}, u32[]{:S(2)}) collective-permute-start(bf16[256]{0:T(256)(128)(2,1)S(1)} %collective-permute-done.2), channel_id=1, source_target_pairs={{0,1},{1,2},{2,3},{3,4},{4,5},{5,6},{6,7},{7,0},{8,9},{9,10},{10,1... | collective-permute-start | bytes 1544 | tf_op jit(solution)/shard_map/ppermute | solution.py:13
  50.8 5.5 %collective-permute-start.5 = (bf16[256]{0:T(256)(128)(2,1)S(1)}, bf16[256]{0:T(256)(128)(2,1)S(1)}, u32[]{:S(2)}, u32[]{:S(2)}) collective-permute-start(bf16[256]{0:T(256)(128)(2,1)S(1)} %collective-permute-done.3), channel_id=1, source_target_pairs={{0,7},{1,0},{2,1},{3,2},{4,3},{5,4},{6,5},{7,6},{8,15},{9,8},{10,9... | collective-permute-start | bytes 1544 | tf_op jit(solution)/shard_map/ppermute | solution.py:16
  55.3 4.8 %collective-permute-start.6 = (bf16[256]{0:T(256)(128)(2,1)S(1)}, bf16[256]{0:T(256)(128)(2,1)S(1)}, u32[]{:S(2)}, u32[]{:S(2)}) collective-permute-start(bf16[256]{0:T(256)(128)(2,1)S(1)} %collective-permute-done.4), channel_id=1, source_target_pairs={{0,1},{1,2},{2,3},{3,4},{4,5},{5,6},{6,7},{7,0},{8,9},{9,10},{10,1... | collective-permute-start | bytes 1544 | tf_op jit(solution)/shard_map/ppermute | solution.py:13
  92.1 7.0 %copy-start = (f32[2048,1024]{1,0:T(8,128)S(1)}, f32[2048,1024]{1,0:T(8,128)}, u32[]{:S(2)}) copy-start(f32[2048,1024]{1,0:T(8,128)} %get-tuple-element.7) | copy-start | bytes 25165828
Sparse Core Ops, SparseCore 0:
  9.0 24.7 all-gather.2
  103.0 20.7 reduce-scatter.1
